TPU v7x, 1024 devices: a whole 8x8x8 slice. The times are simulated.
1024 devices in a mesh: pipe: 4 (over z_hi), dp: 64 (over x, y), tensor: 4 (over z_lo, core).
Axes of the slice: x: 8, y: 8, z: 8 (z_hi: 4, z_lo: 2; z = z_hi * 2 + z_lo), core: 2. Of those that a mesh axis runs over, the one named last changes fastest.
Arguments:
- up_weight: bfloat16 [4, 2048, 4096], P('pipe', None, 'tensor'), may hold values from -0.125 to 0.125
- down_weight: bfloat16 [4, 2048, 4096], P('pipe', None, 'tensor'), may hold values from -0.09375 to 0.09375
- gate_act: bfloat16 [4, 8192, 4096], P('pipe', 'dp', 'tensor'), may hold values from -0.27734375 to 2.5
- hidden: bfloat16 [4, 8192, 4096], P('pipe', 'dp', 'tensor'), may hold values from -6 to 6
- block_input: bfloat16 [4, 8192, 2048], P('pipe', ('dp', 'tensor')), may hold values from -6 to 6
- norm_gain: float32 [4, 2048], P('pipe'), may hold values from 0.1 to 1.9
- loss_grad: bfloat16 [8192, 2048], P(('dp', 'tensor')), may hold values from -2.5 to 2.5
- moment_one: float32 [4, 2048, 4096], P('pipe', 'dp', 'tensor'), may hold values from -6 to 6
- moment_two: float32 [4, 2048, 4096], P('pipe', 'dp', 'tensor'), may hold values from 1 to 30
Outputs:
- input_grad: bfloat16 [4, 8192, 2048], P('pipe', ('dp', 'tensor'))
- new_moment_one: float32 [4, 2048, 4096], P('pipe', 'dp', 'tensor')
- new_moment_two: float32 [4, 2048, 4096], P('pipe', 'dp', 'tensor')
- new_down_weight: float32 [4, 2048, 4096], P('pipe', 'dp', 'tensor')
All inputs are finite; a program needn't handle non-finite values.
Results may differ from a plain program's by a relative error of at most 0.028.
Values may be sent and summed in bfloat16 or wider, within the bound.
A program may use at most 64 MiB of HBM per device.

v0:
```python
import jax
import jax.numpy as jnp
from jax import lax
from jax.sharding import PartitionSpec as P

EPS_NORM = 1e-05
EPS_ADAM = 1e-08
BETA_ONE = 0.9
BETA_TWO = 0.95
RATE = 0.01
DECAY = 0.1
CORRECT_ONE = 1.0 - 0.9**10
CORRECT_TWO = 1.0 - 0.95**10


def shifted(shard, axis, by):
    size = lax.axis_size(axis)
    pairs = [(i, i + by) for i in range(size) if 0 <= i + by < size]
    return lax.ppermute(shard, axis, pairs)


def rounded(value):
    return lax.optimization_barrier(value.astype(jnp.bfloat16)).astype(jnp.float32)


def on_device(
    up_weight,
    down_weight,
    gate_act,
    hidden,
    block_input,
    norm_gain,
    loss_grad,
    moment_one,
    moment_two,
):
    w_up = up_weight[0]
    w_down = down_weight[0]
    gates = gate_act[0].astype(jnp.float32)
    saved = hidden[0]
    rows_in = block_input[0].astype(jnp.float32)
    gain = norm_gain[0][None, :]
    sections = lax.axis_size("pipe")
    segment = lax.axis_index("pipe")
    tok_share = rows_in.shape[0]
    model_width = rows_in.shape[1]
    unit_width = w_up.shape[1]
    inverse_rms = lax.rsqrt(jnp.mean(rows_in * rows_in, axis=-1, keepdims=True) + EPS_NORM)
    upstream0 = jnp.where(segment == sections - 1, loss_grad, jnp.zeros_like(loss_grad))
    kept_dx0 = jnp.zeros_like(loss_grad)
    kept_full0 = jnp.zeros((tok_share * lax.axis_size("tensor"), model_width), jnp.bfloat16)

    def section_step(layer_step, carry):
        upstream, kept_dx, kept_full = carry
        active = segment == sections - 1 - layer_step
        full_grad = lax.all_gather(upstream, "tensor", axis=0, tiled=True)
        unit_grad = lax.cond(
            active,
            lambda: (jnp.dot(full_grad, w_down, preferred_element_type=jnp.float32) * gates).astype(
                jnp.bfloat16
            ),
            lambda: jnp.zeros((full_grad.shape[0], unit_width), jnp.bfloat16),
        )
        normed = lax.psum_scatter(
            lax.cond(
                active,
                lambda: lax.dot_general(
                    unit_grad, w_up, (((1,), (1,)), ((), ())), preferred_element_type=jnp.float32
                ),
                lambda: jnp.zeros((tok_share * lax.axis_size("tensor"), model_width), jnp.float32),
            ).astype(jnp.bfloat16),
            "tensor",
            scatter_dimension=0,
            tiled=True,
        ).astype(jnp.float32)
        scaled = normed * gain
        mean_term = jnp.mean(rows_in * scaled, axis=-1, keepdims=True)
        out_grad = (
            upstream.astype(jnp.float32)
            + inverse_rms * scaled
            - rows_in * inverse_rms**3 * mean_term
        ).astype(jnp.bfloat16)
        kept_dx = jnp.where(active, out_grad, kept_dx)
        kept_full = jnp.where(active, full_grad, kept_full)
        arrived = shifted(out_grad, "pipe", -1)
        upstream = jnp.where(segment == sections - 2 - layer_step, arrived, upstream)
        return (upstream, kept_dx, kept_full)

    final_up, kept_dx, kept_full = lax.fori_loop(
        0, sections, section_step, (upstream0, kept_dx0, kept_full0)
    )
    owners = lax.axis_size("dp")
    row_share = model_width // owners
    partial_grad = lax.dot_general(
        kept_full, saved, (((0,), (0,)), ((), ())), preferred_element_type=jnp.float32
    )
    gradient = lax.psum_scatter(rounded(partial_grad), "dp", scatter_dimension=0, tiled=True)
    owner = lax.axis_index("dp")
    current = lax.dynamic_slice_in_dim(w_down, owner * row_share, row_share, 0).astype(jnp.float32)
    first = BETA_ONE * moment_one[0] + (1.0 - BETA_ONE) * gradient
    second = BETA_TWO * moment_two[0] + (1.0 - BETA_TWO) * gradient * gradient
    direction = first / CORRECT_ONE / (jnp.sqrt(second / CORRECT_TWO) + EPS_ADAM) + DECAY * current
    updated = current - RATE * direction
    return (kept_dx[None], first[None], second[None], updated[None])


def solution(mesh):
    in_specs = (
        P("pipe", None, "tensor"),
        P("pipe", None, "tensor"),
        P("pipe", "dp", "tensor"),
        P("pipe", "dp", "tensor"),
        P("pipe", ("dp", "tensor"), None),
        P("pipe", None),
        P(("dp", "tensor"), None),
        P("pipe", "dp", "tensor"),
        P("pipe", "dp", "tensor"),
    )
    out_specs = (
        P("pipe", ("dp", "tensor"), None),
        P("pipe", "dp", "tensor"),
        P("pipe", "dp", "tensor"),
        P("pipe", "dp", "tensor"),
    )
    return jax.shard_map(
        on_device, mesh=mesh, in_specs=in_specs, out_specs=out_specs, check_vma=False
    )
```

profile of v0, /device:TPU:1, one launch (start us, length us, event | category | flops | bytes accessed | tf_op | source)
XLA Modules:
  0.0 511.6 jit_solution(18148377376848230047)
XLA Ops:
  8.0 0.0 copy-start
  8.0 1.1 multiply_reduce_fusion.1
  9.1 0.9 bitcast_convert_fusion.1
  10.1 1.0 bitcast_convert_fusion
  11.1 229.5 %while.20 = (s32[]{:T(128)}, bf16[32,2048]{1,0:T(8,128)(2,1)S(1)}, bf16[32,2048]{1,0:T(8,128)(2,1)S(1)}, bf16[128,2048]{1,0:T(8,128)(2,1)S(1)}, s32[]{:T(128)}, ...) while((s32[]{:T(128)}, bf16[32,2048]{1,0:T(8,128)(2,1)S(1)}, ...), condition=%wide.region_8.9_spmd.clone, body=%wide.region_1.8_spmd.clone.sunk | while | flops 1075576832 | bytes 19055768 | solution.py:89
  11.1 0.0 reduce-scatter.5.cloned.1.call-start
  11.2 20.5 %all_gather.11 = bf16[128,2048]{1,0:T(8,128)(2,1)S(1)} all-gather(bf16[32,2048]{1,0:T(8,128)(2,1)S(1)} %get-tuple-element.461), channel_id=1, replica_groups=mesh['pipe'=4,'dp'=64,'tensor'=4] {'tensor'}, dimensions={0}, use_global_device_ids=true | all-gather | bytes 655360 | tf_op jit(solution)/shard_map/while/body/eval_jaxpr/all_gather | solution.py:56
  31.7 0.0 copy-start.3
  31.7 0.1 conditional.7
  31.8 0.8 copy-done.1
  32.6 0.0 reduce-scatter.5.cloned.1.call-update
  32.6 33.6 %reduce-scatter.5.cloned.1.call-done = bf16[32,2048]{1,0:T(8,128)(2,1)} async-done(((bf16[128,2048]{1,0:T(8,128)(2,1)}), bf16[32,2048]{1,0:T(8,128)(2,1)}) %reduce-scatter.5.cloned.1.call-update) | async-done | bytes 131088 | tf_op jit(solution)/shard_map/while/body/eval_jaxpr/reduce_scatter | solution.py:64
  66.2 1.0 multiply_reduce_fusion.3
  67.3 1.1 select_select_fusion.4
  68.3 1.3 collective-permute-start
  69.6 0.2 select_select_fusion.5
  69.9 9.8 %collective-permute-done = bf16[32,2048]{1,0:T(8,128)(2,1)S(1)} collective-permute-done((bf16[32,2048]{1,0:T(8,128)(2,1)S(1)}, bf16[32,2048]{1,0:T(8,128)(2,1)S(1)}, u32[]{:S(2)}, u32[]{:S(2)}) %collective-permute-start) | collective-permute-done | bytes 131104 | tf_op jit(solution)/shard_map/while/body/eval_jaxpr/ppermute | solution.py:19
  79.7 0.0 reduce-scatter.5.cloned.1.call-start
  79.8 7.3 %all_gather.11 = bf16[128,2048]{1,0:T(8,128)(2,1)S(1)} all-gather(bf16[32,2048]{1,0:T(8,128)(2,1)S(1)} %get-tuple-element.461), channel_id=1, replica_groups=mesh['pipe'=4,'dp'=64,'tensor'=4] {'tensor'}, dimensions={0}, use_global_device_ids=true | all-gather | bytes 655360 | tf_op jit(solution)/shard_map/while/body/eval_jaxpr/all_gather | solution.py:56
  87.1 0.0 copy-start.3
  87.1 0.1 conditional.7
  87.2 0.8 copy-done.1
  88.0 0.0 reduce-scatter.5.cloned.1.call-update
  88.0 34.0 %reduce-scatter.5.cloned.1.call-done = bf16[32,2048]{1,0:T(8,128)(2,1)} async-done(((bf16[128,2048]{1,0:T(8,128)(2,1)}), bf16[32,2048]{1,0:T(8,128)(2,1)}) %reduce-scatter.5.cloned.1.call-update) | async-done | bytes 131088 | tf_op jit(solution)/shard_map/while/body/eval_jaxpr/reduce_scatter | solution.py:64
  122.0 1.0 multiply_reduce_fusion.3
  123.1 1.1 select_select_fusion.4
  124.1 1.3 collective-permute-start
  125.4 0.2 select_select_fusion.5
  125.6 9.7 %collective-permute-done = bf16[32,2048]{1,0:T(8,128)(2,1)S(1)} collective-permute-done((bf16[32,2048]{1,0:T(8,128)(2,1)S(1)}, bf16[32,2048]{1,0:T(8,128)(2,1)S(1)}, u32[]{:S(2)}, u32[]{:S(2)}) %collective-permute-start) | collective-permute-done | bytes 131104 | tf_op jit(solution)/shard_map/while/body/eval_jaxpr/ppermute | solution.py:19
  135.4 0.0 reduce-scatter.5.cloned.1.call-start
  135.5 7.3 %all_gather.11 = bf16[128,2048]{1,0:T(8,128)(2,1)S(1)} all-gather(bf16[32,2048]{1,0:T(8,128)(2,1)S(1)} %get-tuple-element.461), channel_id=1, replica_groups=mesh['pipe'=4,'dp'=64,'tensor'=4] {'tensor'}, dimensions={0}, use_global_device_ids=true | all-gather | bytes 655360 | tf_op jit(solution)/shard_map/while/body/eval_jaxpr/all_gather | solution.py:56
  142.8 0.0 copy-start.3
  142.8 0.1 conditional.7
  142.9 0.8 copy-done.1
  143.7 0.0 reduce-scatter.5.cloned.1.call-update
  143.7 32.7 %reduce-scatter.5.cloned.1.call-done = bf16[32,2048]{1,0:T(8,128)(2,1)} async-done(((bf16[128,2048]{1,0:T(8,128)(2,1)}), bf16[32,2048]{1,0:T(8,128)(2,1)}) %reduce-scatter.5.cloned.1.call-update) | async-done | bytes 131088 | tf_op jit(solution)/shard_map/while/body/eval_jaxpr/reduce_scatter | solution.py:64
  176.4 1.0 multiply_reduce_fusion.3
  177.5 1.1 select_select_fusion.4
  178.5 1.3 collective-permute-start
  179.8 0.2 select_select_fusion.5
  180.1 9.8 %collective-permute-done = bf16[32,2048]{1,0:T(8,128)(2,1)S(1)} collective-permute-done((bf16[32,2048]{1,0:T(8,128)(2,1)S(1)}, bf16[32,2048]{1,0:T(8,128)(2,1)S(1)}, u32[]{:S(2)}, u32[]{:S(2)}) %collective-permute-start) | collective-permute-done | bytes 131104 | tf_op jit(solution)/shard_map/while/body/eval_jaxpr/ppermute | solution.py:19
  189.9 0.0 reduce-scatter.5.cloned.1.call-start
  190.0 7.3 %all_gather.11 = bf16[128,2048]{1,0:T(8,128)(2,1)S(1)} all-gather(bf16[32,2048]{1,0:T(8,128)(2,1)S(1)} %get-tuple-element.461), channel_id=1, replica_groups=mesh['pipe'=4,'dp'=64,'tensor'=4] {'tensor'}, dimensions={0}, use_global_device_ids=true | all-gather | bytes 655360 | tf_op jit(solution)/shard_map/while/body/eval_jaxpr/all_gather | solution.py:56
  197.2 2.9 conditional.6
  197.2 2.9 fusion
  200.2 0.0 copy-start.3
  200.2 3.7 conditional.7
  200.2 3.7 fusion.8
  203.9 0.8 copy-done.1
  204.7 0.0 reduce-scatter.5.cloned.1.call-update
  204.7 22.5 %reduce-scatter.5.cloned.1.call-done = bf16[32,2048]{1,0:T(8,128)(2,1)} async-done(((bf16[128,2048]{1,0:T(8,128)(2,1)}), bf16[32,2048]{1,0:T(8,128)(2,1)}) %reduce-scatter.5.cloned.1.call-update) | async-done | bytes 131088 | tf_op jit(solution)/shard_map/while/body/eval_jaxpr/reduce_scatter | solution.py:64
  227.2 1.0 multiply_reduce_fusion.3
  228.3 1.1 select_select_fusion.4
  229.3 1.3 collective-permute-start
  230.6 0.2 select_select_fusion.5
  230.9 9.7 %collective-permute-done = bf16[32,2048]{1,0:T(8,128)(2,1)S(1)} collective-permute-done((bf16[32,2048]{1,0:T(8,128)(2,1)S(1)}, bf16[32,2048]{1,0:T(8,128)(2,1)S(1)}, u32[]{:S(2)}, u32[]{:S(2)}) %collective-permute-start) | collective-permute-done | bytes 131104 | tf_op jit(solution)/shard_map/while/body/eval_jaxpr/ppermute | solution.py:19
  240.6 0.0 copy-start.2
  240.6 0.0 reduce-scatter.3.cloned.1.call-start
  240.7 1.3 convolution_convert_fusion
  242.0 0.0 copy-done.2
  242.0 4.3 convert_element_type.78
  246.2 0.0 reduce-scatter.3.cloned.1.call-update
  246.3 256.5 %reduce-scatter.3.cloned.1.call-done = f32[32,1024]{1,0:T(8,128)} async-done(((f32[2048,1024]{1,0:T(8,128)}), f32[32,1024]{1,0:T(8,128)}) %reduce-scatter.3.cloned.1.call-update) | async-done | bytes 131088 | tf_op jit(solution)/shard_map/reduce_scatter | solution.py:97
  502.8 1.7 fusion.4
  (35 shorter events, 0.5 us)
Async XLA Ops:
  8.0 232.7 %copy-start = (bf16[1,128,1024]{2,1,0:T(8,128)(2,1)S(1)}, bf16[1,128,1024]{2,1,0:T(8,128)(2,1)}, u32[]{:S(2)}) copy-start(bf16[1,128,1024]{2,1,0:T(8,128)(2,1)} %param.18) | copy-start | bytes 786436
  11.1 55.1 %reduce-scatter.5.cloned.1.call-start = ((), (), s32[]{:S(2)}) async-start(), calls=%async_computation.3 | async-start | bytes 655360 | tf_op jit(solution)/shard_map/while/body/eval_jaxpr/reduce_scatter | solution.py:64
  31.7 34.6 %copy-start.3 = (f32[1,2048]{1,0:T(1,128)S(1)}, f32[1,2048]{1,0:T(1,128)}, u32[]{:S(2)}) copy-start(f32[1,2048]{1,0:T(1,128)} %get-tuple-element.485) | copy-start | bytes 24580 | tf_op jit(solution)/shard_map/while
  31.8 0.8 copy-start.1
  68.3 11.3 %collective-permute-start = (bf16[32,2048]{1,0:T(8,128)(2,1)S(1)}, bf16[32,2048]{1,0:T(8,128)(2,1)S(1)}, u32[]{:S(2)}, u32[]{:S(2)}) collective-permute-start(bf16[32,2048]{1,0:T(8,128)(2,1)S(1)} %get-tuple-element.442), channel_id=1, source_target_pairs={{256,0},{512,256},{768,512},{257,1},{513,257},{769,513},{258,2},{5... | collective-permute-start | bytes 393224 | tf_op jit(solution)/shard_map/while/body/eval_jaxpr/ppermute | solution.py:19
  79.7 42.3 %reduce-scatter.5.cloned.1.call-start = ((), (), s32[]{:S(2)}) async-start(), calls=%async_computation.3 | async-start | bytes 655360 | tf_op jit(solution)/shard_map/while/body/eval_jaxpr/reduce_scatter | solution.py:64
  87.1 34.9 %copy-start.3 = (f32[1,2048]{1,0:T(1,128)S(1)}, f32[1,2048]{1,0:T(1,128)}, u32[]{:S(2)}) copy-start(f32[1,2048]{1,0:T(1,128)} %get-tuple-element.485) | copy-start | bytes 24580 | tf_op jit(solution)/shard_map/while
  87.2 0.8 copy-start.1
  124.1 11.3 %collective-permute-start = (bf16[32,2048]{1,0:T(8,128)(2,1)S(1)}, bf16[32,2048]{1,0:T(8,128)(2,1)S(1)}, u32[]{:S(2)}, u32[]{:S(2)}) collective-permute-start(bf16[32,2048]{1,0:T(8,128)(2,1)S(1)} %get-tuple-element.442), channel_id=1, source_target_pairs={{256,0},{512,256},{768,512},{257,1},{513,257},{769,513},{258,2},{5... | collective-permute-start | bytes 393224 | tf_op jit(solution)/shard_map/while/body/eval_jaxpr/ppermute | solution.py:19
  135.4 41.0 %reduce-scatter.5.cloned.1.call-start = ((), (), s32[]{:S(2)}) async-start(), calls=%async_computation.3 | async-start | bytes 655360 | tf_op jit(solution)/shard_map/while/body/eval_jaxpr/reduce_scatter | solution.py:64
  142.8 33.6 %copy-start.3 = (f32[1,2048]{1,0:T(1,128)S(1)}, f32[1,2048]{1,0:T(1,128)}, u32[]{:S(2)}) copy-start(f32[1,2048]{1,0:T(1,128)} %get-tuple-element.485) | copy-start | bytes 24580 | tf_op jit(solution)/shard_map/while
  142.9 0.8 copy-start.1
  178.5 11.3 %collective-permute-start = (bf16[32,2048]{1,0:T(8,128)(2,1)S(1)}, bf16[32,2048]{1,0:T(8,128)(2,1)S(1)}, u32[]{:S(2)}, u32[]{:S(2)}) collective-permute-start(bf16[32,2048]{1,0:T(8,128)(2,1)S(1)} %get-tuple-element.442), channel_id=1, source_target_pairs={{256,0},{512,256},{768,512},{257,1},{513,257},{769,513},{258,2},{5... | collective-permute-start | bytes 393224 | tf_op jit(solution)/shard_map/while/body/eval_jaxpr/ppermute | solution.py:19
  189.9 37.3 %reduce-scatter.5.cloned.1.call-start = ((), (), s32[]{:S(2)}) async-start(), calls=%async_computation.3 | async-start | bytes 655360 | tf_op jit(solution)/shard_map/while/body/eval_jaxpr/reduce_scatter | solution.py:64
  200.2 27.1 %copy-start.3 = (f32[1,2048]{1,0:T(1,128)S(1)}, f32[1,2048]{1,0:T(1,128)}, u32[]{:S(2)}) copy-start(f32[1,2048]{1,0:T(1,128)} %get-tuple-element.485) | copy-start | bytes 24580 | tf_op jit(solution)/shard_map/while
  203.9 0.8 copy-start.1
  229.3 11.2 %collective-permute-start = (bf16[32,2048]{1,0:T(8,128)(2,1)S(1)}, bf16[32,2048]{1,0:T(8,128)(2,1)S(1)}, u32[]{:S(2)}, u32[]{:S(2)}) collective-permute-start(bf16[32,2048]{1,0:T(8,128)(2,1)S(1)} %get-tuple-element.442), channel_id=1, source_target_pairs={{256,0},{512,256},{768,512},{257,1},{513,257},{769,513},{258,2},{5... | collective-permute-start | bytes 393224 | tf_op jit(solution)/shard_map/while/body/eval_jaxpr/ppermute | solution.py:19
  240.6 1.4 copy-start.2
  240.6 262.1 %reduce-scatter.3.cloned.1.call-start = ((), (), s32[]{:S(2)}) async-start(), calls=%async_computation.2 | async-start | bytes 8519680 | tf_op jit(solution)/shard_map/reduce_scatter | solution.py:97
  246.2 256.5 %copy-start.4 = (f32[1,32,1024]{2,1,0:T(8,128)S(1)}, f32[1,32,1024]{2,1,0:T(8,128)}, u32[]{:S(2)}) copy-start(f32[1,32,1024]{2,1,0:T(8,128)} %param.22) | copy-start | bytes 393220
  246.2 256.5 %copy-start.5 = (f32[1,32,1024]{2,1,0:T(8,128)S(1)}, f32[1,32,1024]{2,1,0:T(8,128)}, u32[]{:S(2)}) copy-start(f32[1,32,1024]{2,1,0:T(8,128)} %param.23) | copy-start | bytes 393220
Sparse Core Ops, SparseCore 0:
  32.7 33.4 reduce-scatter.4
  88.1 33.8 reduce-scatter.4
  143.8 32.5 reduce-scatter.4
  204.8 22.3 reduce-scatter.4
Sparse Core Ops, SparseCore 1:
  246.4 256.3 reduce-scatter.2
where the time goes:
time: 516 us; the launch traced here: 512 us
  waiting for transfers between devices  418 us (81%)
  blocking collectives  42.3 us (8%)
  other arithmetic  18.4 us (4%)
  between operations  15.3 us (3%)
  matrix products  7.86 us (2%)
  starting transfers between devices  5.38 us (1%)
    reduce_scatter x1, waiting for transfers between devices, on_device(): lax.psum_scatter(rounded(partial_grad), 'dp', scatter_dimension=0, tiled=...  256 us
    reduce_scatter x4, waiting for transfers between devices, section_step(): lax.psum_scatter(lax.cond(active, lambda: lax.dot_general(unit_grad, w_up...  123 us
    all_gather x4, blocking collectives, section_step(): full_grad = lax.all_gather(upstream, 'tensor', axis=0, tiled=True)  42.3 us
    ppermute x4, waiting for transfers between devices, shifted(): return lax.ppermute(shard, axis, pairs)  39 us
  transfers between devices with their start and end apart: 9, of which 9 were waited for; matrix products, arithmetic and copies ran while one was open for 0% of the time, Pallas kernels for 0%

commit v1 on v0

v1 whole, which is shorter than its diff:
```python
import functools

import jax
import jax.numpy as jnp
from jax import lax
from jax.experimental import pallas as pl
from jax.experimental.pallas import tpu as pltpu
from jax.sharding import PartitionSpec as P

EPS_NORM = 1e-05
EPS_ADAM = 1e-08
BETA_ONE = 0.9
BETA_TWO = 0.95
RATE = 0.01
DECAY = 0.1
CORRECT_ONE = 1.0 - 0.9**10
CORRECT_TWO = 1.0 - 0.95**10

MESH = pl.DeviceIdType.MESH
F32 = jnp.float32
BF16 = jnp.bfloat16


def kernel(
    grid_x, grid_y, chunks,
    w_up, w_down, gate_act, hidden, block_input, norm_gain, loss_grad, moment_one, moment_two,
    out_dx, out_first, out_second, out_weight,
    wd, wu, gates, rows_in, gain, mom1, mom2,
    up, up_t, acc, unit, part, half_send, half_recv, quarter_send, quarter_recv, scaled, dx,
    hid_a, hid_b, upt_a, upt_b, grad_a, grad_b, gsend_a, gsend_b, grecv_a, grecv_b,
    first_v, second_v, weight_v,
    sem_in, sem_out, sem_block, sem_mate, sem_half, sem_quarter,
    sem_hid_a, sem_hid_b, sem_upt_a, sem_upt_b, sem_mate_a, sem_mate_b, sem_grad_a, sem_grad_b,
    send_fwd, send_mate, send_half, send_quarter, send_dx,
    send_hid, send_upt, send_upt_mate, send_grad,
):
    pipe = lax.axis_index("pipe")
    owner = lax.axis_index("dp")
    tensor = lax.axis_index("tensor")
    sections = lax.axis_size("pipe")
    x = lax.div(owner, grid_y)
    y = lax.rem(owner, grid_y)
    chip = lax.div(tensor, 2)
    core = lax.rem(tensor, 2)
    mate = {"tensor": chip * 2 + 1 - core}
    across = {"tensor": (1 - chip) * 2 + core}
    last = pipe == sections - 1
    tokens, width = up.shape
    share = tokens // 4
    units = wd.shape[1]
    row_share = width // (grid_x * grid_y)
    span = width // chunks
    cols = units // 2

    def x_peer(k):
        return lax.rem(x + k, grid_x)

    def y_peer(k):
        return lax.rem(y + k, grid_y)

    def aligned(value, step):
        return pl.multiple_of(value * step, step)

    def remote(src, dst, send, recv, device):
        return pltpu.make_async_remote_copy(
            src_ref=src, dst_ref=dst, send_sem=send, recv_sem=recv, device_id=device, device_id_type=MESH
        )

    sent = []

    def start(copy, when=None):
        if when is None:
            copy.start()
        else:
            pl.when(when)(copy.start)
        sent.append((copy, when))

    order = [(0, 0), (0, 1), (1, 0), (1, 1)]

    def token_rows(c, z):
        return pl.ds((z * 2 + c) * share, share)

    loads = {}

    def load(name, src, dst, when=None):
        copy = pltpu.make_async_copy(src, dst, sem_in.at[len(loads)])
        loads[name] = copy
        if when is None:
            copy.start()
        else:
            pl.when(when)(copy.start)

    my_rows = pl.ds(aligned(core * 2 + chip, share), share)
    load("loss", loss_grad, up.at[my_rows], last)
    load("wd", w_down.at[0], wd)
    load("rows", block_input.at[0], rows_in)
    load("gain", norm_gain, gain)
    for n, (c, z) in enumerate(order):
        load(f"gate{n}", gate_act.at[0, token_rows(c, z)], gates.at[pl.ds(n * share, share)])
    load("wu", w_up.at[0], wu)
    for n, (c, z) in enumerate(order):
        src = hidden.at[0, token_rows(c, z)]
        load(f"hida{n}", src.at[:, pl.ds(0, cols)], hid_a.at[x, pl.ds(n * share, share)])
        load(f"hidb{n}", src.at[:, pl.ds(cols, cols)], hid_b.at[y, pl.ds(n * share, share)])
    load("mom1", moment_one.at[0], mom1)
    load("mom2", moment_two.at[0], mom2)

    barrier = pltpu.get_barrier_semaphore()

    def greet(device):
        pl.semaphore_signal(barrier, inc=1, device_id=device, device_id_type=MESH)

    greet(mate)
    greet(across)

    @pl.when(jnp.logical_and(pipe < sections - 1, chip == 1))
    def _():
        greet({"pipe": pipe + 1, "tensor": core})
        greet({"pipe": pipe + 1, "tensor": 2 + core})

    for k in range(1, grid_x):
        greet({"dp": x_peer(k) * grid_y + y})
    for k in range(1, grid_y):
        greet({"dp": x * grid_y + y_peer(k)})

    @pl.when(pipe == 0)
    def _():
        pl.semaphore_wait(barrier, grid_x + grid_y)

    @pl.when(pipe > 0)
    def _():
        pl.semaphore_wait(barrier, grid_x + grid_y + 1)

    pl.when(last)(loads["loss"].wait)

    def columns(j):
        return pl.ds(j * span, span)

    def block(z, c, j):
        return up.at[pl.ds(aligned(c * 2 + z, share), share), columns(j)]

    for z in range(2):
        for j in range(chunks):
            ref = block(z, core, j)
            start(
                remote(ref, ref, send_fwd.at[z, j], sem_block.at[z, j], across),
                jnp.logical_and(last, chip == z),
            )
            sent.pop()

    for n in range(4):
        loads[f"hida{n}"].wait()
        loads[f"hidb{n}"].wait()
    for k in range(1, grid_x):
        ref = hid_a.at[x]
        start(remote(ref, ref, send_hid.at[k], sem_hid_a.at[x], {"dp": x_peer(k) * grid_y + y}))
    for k in range(1, grid_y):
        ref = hid_b.at[y]
        start(remote(ref, ref, send_hid.at[grid_x + k], sem_hid_b.at[y], {"dp": x * grid_y + y_peer(k)}))

    for name in ("wd", "rows", "gain", "wu", "mom1", "mom2"):
        loads[name].wait()
    for n in range(4):
        loads[f"gate{n}"].wait()

    source = rows_in[...].astype(F32)
    inverse_rms = lax.rsqrt(jnp.mean(source * source, axis=-1, keepdims=True) + EPS_NORM)

    def pass_on(j):
        for z in range(2):
            ref = block(z, core, j)
            forward = remote(ref, ref, send_fwd.at[z, j], sem_block.at[z, j], across)
            own = jnp.logical_and(last, chip == z)
            pl.when(jnp.logical_not(own))(forward.wait_recv)
            relay = jnp.logical_and(jnp.logical_not(last), chip == 1)
            pl.when(relay)(forward.start)
            sent.append((forward, jnp.logical_or(own, relay)))
            start(remote(ref, ref, send_mate.at[z, j], sem_mate.at[z, j], mate))

    def multiply(j):
        for z in range(2):
            ref = block(z, 1 - core, j)
            remote(ref, ref, send_mate.at[z, j], sem_mate.at[z, j], mate).wait_recv()
        left = up[:, columns(j)]
        for n in range(0, units, 256):
            right = pl.ds(n, 256)
            term = jnp.dot(left, wd[columns(j), right], preferred_element_type=F32)
            if j > 0:
                term = term + acc[:, right]
            if j < chunks - 1:
                acc[:, right] = term
            else:
                unit[:, right] = (term * gates[:, right].astype(F32)).astype(BF16)

    per = grid_x // chunks

    def turn(j):
        turned = up[:, columns(j)].astype(F32).T.astype(BF16)
        up_t[pl.ds(j * per, per)] = turned.reshape(per, grid_y, row_share, tokens)

    pass_on(0)
    for j in range(chunks):
        if j + 1 < chunks:
            pass_on(j + 1)
        multiply(j)
        if j + 1 < chunks:
            turn(j)

    mates_half = pl.ds(aligned(1 - core, 2 * share), 2 * share)
    far = pl.ds(aligned(core * 2 + 1 - chip, share), share)
    far_half = pl.ds(aligned(1 - chip, share), share)
    near_half = pl.ds(aligned(chip, share), share)

    def second(i):
        for n in range(i * span, (i + 1) * span, 256):
            part[:, pl.ds(n, 256)] = lax.dot_general(
                unit[...], wu[pl.ds(n, 256), :], (((1,), (1,)), ((), ())), preferred_element_type=F32
            )
        half_send[:, columns(i)] = part[mates_half, columns(i)].astype(BF16)
        start(
            remote(
                half_send.at[:, columns(i)], half_recv.at[:, columns(i)], send_half.at[i], sem_half.at[i], mate
            )
        )

    def chip_sum(i):
        got = half_recv.at[:, columns(i)]
        remote(got, got, send_half.at[i], sem_half.at[i], mate).wait_recv()
        quarter_send[:, columns(i)] = (
            part[far, columns(i)] + half_recv[far_half, columns(i)].astype(F32)
        ).astype(BF16)
        start(
            remote(
                quarter_send.at[:, columns(i)],
                quarter_recv.at[:, columns(i)],
                send_quarter.at[i],
                sem_quarter.at[i],
                across,
            )
        )

    second(0)
    turn(chunks - 1)

    half_y, half_x = grid_y // 2, grid_x // 2
    for k in range(1, grid_x):
        start(
            remote(
                up_t.at[x_peer(k), pl.ds(core * half_y, half_y)],
                upt_a.at[pl.ds(core * half_y, half_y), :, pl.ds(aligned(x, tokens), tokens)],
                send_upt.at[k],
                sem_upt_a.at[x],
                {"dp": x_peer(k) * grid_y + y},
            )
        )
    for k in range(1, grid_y):
        start(
            remote(
                up_t.at[pl.ds(core * half_x, half_x), y_peer(k)],
                upt_b.at[pl.ds(core * half_x, half_x), :, pl.ds(aligned(y, tokens), tokens)],
                send_upt.at[grid_x + k],
                sem_upt_b.at[y],
                {"dp": x * grid_y + y_peer(k)},
            )
        )

    for i in range(1, chunks):
        second(i)
        chip_sum(i - 1)
    chip_sum(chunks - 1)

    total = jnp.zeros((share, 1), F32)
    for i in range(chunks):
        got = quarter_recv.at[:, columns(i)]
        remote(got, got, send_quarter.at[i], sem_quarter.at[i], across).wait_recv()
        normed = (
            part[my_rows, columns(i)]
            + half_recv[near_half, columns(i)].astype(F32)
            + quarter_recv[:, columns(i)].astype(F32)
        )
        value = normed * gain[:, columns(i)]
        scaled[:, columns(i)] = value
        total = total + jnp.sum(rows_in[:, columns(i)].astype(F32) * value, axis=-1, keepdims=True)
    slope = inverse_rms * inverse_rms * inverse_rms * (total / width)
    for i in range(chunks):
        dx[:, columns(i)] = (
            up[my_rows, columns(i)].astype(F32)
            + inverse_rms * scaled[:, columns(i)]
            - rows_in[:, columns(i)].astype(F32) * slope
        ).astype(BF16)
        start(
            remote(
                dx.at[:, columns(i)],
                up.at[my_rows, columns(i)],
                send_dx.at[i],
                sem_block.at[chip, i],
                {"pipe": jnp.maximum(pipe - 1, 0), "tensor": 2 + core},
            ),
            pipe > 0,
        )
    outs = [pltpu.make_async_copy(dx, out_dx.at[0], sem_out.at[0])]
    outs[0].start()

    upt_a[:, :, pl.ds(aligned(x, tokens), tokens)] = up_t[x]
    upt_b[:, :, pl.ds(aligned(y, tokens), tokens)] = up_t[:, y]

    def collect(slots, sem, mate_sem, send, half, me, size):
        here = pl.ds(core * half, half)
        there = pl.ds((1 - core) * half, half)
        for k in range(size - 1, 0, -1):
            other = lax.rem(me + k, size)
            lane = pl.ds(aligned(other, tokens), tokens)
            mine = slots.at[here, :, lane]
            copy = remote(mine, mine, send.at[k], sem.at[other], mate)
            copy.wait_recv()
            start(remote(mine, mine, send.at[k], mate_sem.at[other], mate))
        for k in range(size - 1, 0, -1):
            other = lax.rem(me + k, size)
            lane = pl.ds(aligned(other, tokens), tokens)
            theirs = slots.at[there, :, lane]
            remote(theirs, theirs, send.at[k], mate_sem.at[other], mate).wait_recv()

    def gather_wait(slots, sem, me, size):
        for k in range(1, size):
            other = lax.rem(me + k, size)
            got = slots.at[other]
            remote(got, got, send_hid.at[k], sem.at[other], mate).wait_recv()

    def contract(slots, hid, grad, gsend, size):
        left = slots[...].reshape(size * row_share, slots.shape[2])
        right = hid[...].reshape(hid.shape[0] * tokens, cols)
        for n in range(0, cols, 256):
            wide = min(256, cols)
            term = jnp.dot(left, right[:, n : n + wide], preferred_element_type=F32)
            term = term.reshape(size, row_share, wide)
            grad[:, :, pl.ds(n, wide)] = term
            gsend[:, :, pl.ds(n, wide)] = term.astype(BF16)

    gather_wait(hid_a, sem_hid_a, x, grid_x)
    collect(upt_a, sem_upt_a, sem_mate_a, send_upt_mate.at[0], half_y, x, grid_x)
    contract(upt_a, hid_a, grad_a, gsend_a, grid_y)
    for k in range(1, grid_y):
        start(
            remote(
                gsend_a.at[y_peer(k)], grecv_a.at[y], send_grad.at[k], sem_grad_a.at[y],
                {"dp": x * grid_y + y_peer(k)},
            )
        )
    gather_wait(hid_b, sem_hid_b, y, grid_y)
    collect(upt_b, sem_upt_b, sem_mate_b, send_upt_mate.at[1], half_x, y, grid_y)
    contract(upt_b, hid_b, grad_b, gsend_b, grid_x)
    for k in range(1, grid_x):
        start(
            remote(
                gsend_b.at[x_peer(k)], grecv_b.at[x], send_grad.at[grid_y + k], sem_grad_b.at[x],
                {"dp": x_peer(k) * grid_y + y},
            )
        )

    def update(grad, grecv, sem, me, size, offset):
        gradient = grad[me]
        for k in range(size - 1, 0, -1):
            other = lax.rem(me + k, size)
            got = grecv.at[other]
            remote(got, got, send_grad.at[k], sem.at[other], mate).wait_recv()
            gradient = gradient + grecv[other].astype(F32)
        at = pl.ds(offset, cols)
        current = wd[pl.ds(aligned(owner, row_share), row_share), at].astype(F32)
        one = BETA_ONE * mom1[:, at] + (1.0 - BETA_ONE) * gradient
        two = BETA_TWO * mom2[:, at] + (1.0 - BETA_TWO) * gradient * gradient
        direction = one / CORRECT_ONE / (jnp.sqrt(two / CORRECT_TWO) + EPS_ADAM) + DECAY * current
        first_v[:, at] = one
        second_v[:, at] = two
        weight_v[:, at] = current - RATE * direction

    update(grad_a, grecv_a, sem_grad_a, y, grid_y, 0)
    update(grad_b, grecv_b, sem_grad_b, x, grid_x, cols)
    for n, (value, out) in enumerate(((first_v, out_first), (second_v, out_second), (weight_v, out_weight))):
        copy = pltpu.make_async_copy(value, out.at[0], sem_out.at[1 + n])
        copy.start()
        outs.append(copy)
    for copy in outs:
        copy.wait()
    for copy, when in sent:
        if when is None:
            copy.wait_send()
        else:
            pl.when(when)(copy.wait_send)


def on_device(grid_x, grid_y, chunks, *args):
    w_up, w_down, gate_act, hidden, block_input, norm_gain, loss_grad, moment_one, moment_two = args
    width, units = w_up.shape[1:]
    tokens = gate_act.shape[1]
    share = tokens // 4
    cols = units // 2
    row_share = width // (grid_x * grid_y)
    outs = [
        jax.ShapeDtypeStruct(block_input.shape, BF16),
        *[jax.ShapeDtypeStruct(moment_one.shape, F32) for _ in range(3)],
    ]
    dma = pltpu.SemaphoreType.DMA
    vmem = pltpu.VMEM
    scratch = [
        vmem((width, units), BF16),
        vmem((width, units), BF16),
        vmem((tokens, units), BF16),
        vmem((share, width), BF16),
        vmem((1, width), F32),
        vmem((row_share, units), F32),
        vmem((row_share, units), F32),
        vmem((tokens, width), BF16),
        vmem((grid_x, grid_y, row_share, tokens), BF16),
        vmem((tokens, units), F32),
        vmem((tokens, units), BF16),
        vmem((tokens, width), F32),
        vmem((2 * share, width), BF16),
        vmem((2 * share, width), BF16),
        vmem((share, width), BF16),
        vmem((share, width), BF16),
        vmem((share, width), F32),
        vmem((share, width), BF16),
        vmem((grid_x, tokens, cols), BF16),
        vmem((grid_y, tokens, cols), BF16),
        vmem((grid_y, row_share, grid_x * tokens), BF16),
        vmem((grid_x, row_share, grid_y * tokens), BF16),
        vmem((grid_y, row_share, cols), F32),
        vmem((grid_x, row_share, cols), F32),
        vmem((grid_y, row_share, cols), BF16),
        vmem((grid_x, row_share, cols), BF16),
        vmem((grid_y, row_share, cols), BF16),
        vmem((grid_x, row_share, cols), BF16),
        vmem((row_share, units), F32),
        vmem((row_share, units), F32),
        vmem((row_share, units), F32),
        dma((24,)),
        dma((4,)),
        dma((2, chunks)),
        dma((2, chunks)),
        dma((chunks,)),
        dma((chunks,)),
        dma((grid_x,)),
        dma((grid_y,)),
        dma((grid_x,)),
        dma((grid_y,)),
        dma((grid_x,)),
        dma((grid_y,)),
        dma((grid_y,)),
        dma((grid_x,)),
        dma((2, chunks)),
        dma((2, chunks)),
        dma((chunks,)),
        dma((chunks,)),
        dma((chunks,)),
        dma((grid_x + grid_y,)),
        dma((grid_x + grid_y,)),
        dma((2, max(grid_x, grid_y))),
        dma((grid_x + grid_y,)),
    ]
    anywhere = pl.BlockSpec(memory_space=pl.ANY)
    return pl.pallas_call(
        functools.partial(kernel, grid_x, grid_y, chunks),
        out_shape=outs,
        in_specs=[anywhere] * 9,
        out_specs=[anywhere] * 4,
        scratch_shapes=scratch,
        compiler_params=pltpu.CompilerParams(
            collective_id=0, has_side_effects=True, vmem_limit_bytes=67043328
        ),
    )(*args)


def solution(mesh, grid=(8, 8), chunks=4):
    in_specs = (
        P("pipe", None, "tensor"),
        P("pipe", None, "tensor"),
        P("pipe", "dp", "tensor"),
        P("pipe", "dp", "tensor"),
        P("pipe", ("dp", "tensor"), None),
        P("pipe", None),
        P(("dp", "tensor"), None),
        P("pipe", "dp", "tensor"),
        P("pipe", "dp", "tensor"),
    )
    out_specs = (
        P("pipe", ("dp", "tensor"), None),
        P("pipe", "dp", "tensor"),
        P("pipe", "dp", "tensor"),
        P("pipe", "dp", "tensor"),
    )
    return jax.shard_map(
        functools.partial(on_device, *grid, chunks),
        mesh=mesh, in_specs=in_specs, out_specs=out_specs, check_vma=False,
    )
```

time: 516 us -> 118 us (0.23)
  waiting for transfers between devices: 418 us -> 0 us
  Pallas kernels: 0 us -> 110 us
  blocking collectives: 42.3 us -> 0 us
  other arithmetic: 18.4 us -> 0 us
  between operations: 15.3 us -> 0.64 us
  matrix products: 7.86 us -> 0 us
  starting transfers between devices: 5.38 us -> 0 us
    reduce_scatter x5 -> x0, waiting for transfers between devices: 379 us -> none  [the longest x1 256 us: on_device(): lax.psum_scatter(rounded(partial_grad), 'dp', scatter_dimension=0, tiled=...]
    pallas_call x0 -> x1, Pallas kernels: none -> 110 us  [on_device(): pl.pallas_call(functools.partial(kernel, grid_x, grid_y, chunks), out_sha...]
    all_gather x4 -> x0, blocking collectives: 42.3 us -> none  [section_step(): full_grad = lax.all_gather(upstream, 'tensor', axis=0, tiled=True)]
    ppermute x4 -> x0, waiting for transfers between devices: 39 us -> none  [shifted(): return lax.ppermute(shard, axis, pairs)]
    dot_general x3 -> x0, matrix products: 7.86 us -> none  [the longest x1 3.69 us: section_step(): lax.dot_general(unit_grad, w_up, (((1,), (1,)), ((), ())), preferred_elem...]
    unnamed x8 -> x4, local copies, waits for them, and re-layouts: 0.02 us -> 6.27 us
    convert_element_type x3 -> x0, other arithmetic: 6.19 us -> none  [the longest x1 4.27 us: rounded(): lax.optimization_barrier(value.astype(jnp.bfloat16)).astype(jnp.float32)]
    reduce_sum x5 -> x0, other arithmetic: 5.26 us -> none  [the longest x4 4.18 us: section_step(): mean_term = jnp.mean(rows_in * scaled, axis=-1, keepdims=True)]
  transfers between devices with their start and end apart: 9 -> 0, of which waited for: 9 -> 0; matrix products, arithmetic and copies ran while one was open for 0% -> 0% of each run, Pallas kernels for 0% -> 0%
where the time goes in v1:
time: 118 us; the launch traced here: 117 us
  Pallas kernels  110 us (93%)
  local copies, waits for them, and re-layouts  6.27 us (5%)
    pallas_call x1, Pallas kernels, on_device(): pl.pallas_call(functools.partial(kernel, grid_x, grid_y, chunks), out_sha...  110 us
    unnamed x4, local copies, waits for them, and re-layouts  6.27 us

profile of v1, /device:TPU:1, one launch (start us, length us, event | category | flops | bytes accessed | tf_op | source)
XLA Modules:
  0.0 117.1 jit_solution(16133368576148331027)
XLA Ops:
  0.6 110.2 %shard_map.120 = (bf16[1,32,2048]{2,1,0:T(8,128)(2,1)}, f32[1,32,1024]{2,1,0:T(8,128)}, f32[1,32,1024]{2,1,0:T(8,128)}, f32[1,32,1024]{2,1,0:T(8,128)}) custom-call(bf16[1,2048,1024]{2,1,0:T(8,128)(2,1)} %w_up.1, bf16[1,2048,1024]{2,1,0:T(8,128)(2,1)} %w_down.1, bf16[1,128,1024]{2,1,0:T(8,128)(2,1)} %gate_act.1, bf16[1,128,1024]{2,1,0:T(8,128)(2,1)} %hidden.1, ...), custom_call_target="tpu_custom_call" | custom-call | tf_op jit(solution)/shard_map/pallas_call | solution.py:461
  110.9 1.6 %copy.17 = bf16[1,32,2048]{2,1,0:T(8,128)(2,1)} copy(bf16[1,32,2048]{2,1,0:T(8,128)(2,1)} %get-tuple-element.8) | data formatting | bytes 262144
  112.4 1.6 %copy.18 = f32[1,32,1024]{2,1,0:T(8,128)} copy(f32[1,32,1024]{2,1,0:T(8,128)} %get-tuple-element.9) | data formatting | bytes 262144
  114.0 1.6 %copy.19 = f32[1,32,1024]{2,1,0:T(8,128)} copy(f32[1,32,1024]{2,1,0:T(8,128)} %get-tuple-element.10) | data formatting | bytes 262144
  115.6 1.6 %copy.20 = f32[1,32,1024]{2,1,0:T(8,128)} copy(f32[1,32,1024]{2,1,0:T(8,128)} %get-tuple-element.11) | data formatting | bytes 262144

commit v2 on v1

v2 whole, which is shorter than its diff:
```python
import functools

import jax
import jax.numpy as jnp
from jax import lax
from jax.experimental import pallas as pl
from jax.experimental.pallas import tpu as pltpu
from jax.sharding import PartitionSpec as P

EPS_NORM = 1e-05
EPS_ADAM = 1e-08
BETA_ONE = 0.9
BETA_TWO = 0.95
RATE = 0.01
DECAY = 0.1
CORRECT_ONE = 1.0 - 0.9**10
CORRECT_TWO = 1.0 - 0.95**10

MESH = pl.DeviceIdType.MESH
F32 = jnp.float32
BF16 = jnp.bfloat16


def far_first(size):
    return sorted(range(1, size), key=lambda k: -min(k, size - k))


def kernel(
    grid_x, grid_y, chunks,
    w_up, w_down, gate_act, hidden, block_input, norm_gain, loss_grad,
    out_dx, out_grad,
    wd, wu, gates, rows_in, gain,
    up, up_t, acc, unit, part, block_send, block_recv, scaled, dx,
    hid_a, hid_b, upt_a, upt_b, grad_a, grad_b, gsend_a, gsend_b, grecv_a, grecv_b, gradient,
    sem_in, sem_out, sem_block, sem_mate, sem_sum,
    sem_hid_a, sem_hid_b, sem_upt_a, sem_upt_b, sem_mate_a, sem_mate_b, sem_grad_a, sem_grad_b,
    send_fwd, send_mate, send_sum, send_dx,
    send_hid, send_upt, send_upt_mate, send_grad,
):
    pipe = lax.axis_index("pipe")
    owner = lax.axis_index("dp")
    tensor = lax.axis_index("tensor")
    sections = lax.axis_size("pipe")
    x = lax.div(owner, grid_y)
    y = lax.rem(owner, grid_y)
    chip = lax.div(tensor, 2)
    core = lax.rem(tensor, 2)
    mate = {"tensor": chip * 2 + 1 - core}
    across = {"tensor": (1 - chip) * 2 + core}
    last = pipe == sections - 1
    streams, stream, width = up.shape
    tokens = streams * stream
    share = tokens // 4
    sub = stream // 4
    units = wd.shape[1]
    row_share = width // (grid_x * grid_y)
    span = width // chunks
    cols = units // 2

    def x_peer(k):
        return lax.rem(x + k, grid_x)

    def y_peer(k):
        return lax.rem(y + k, grid_y)

    def at_x(index):
        return {"dp": index * grid_y + y}

    def at_y(index):
        return {"dp": x * grid_y + index}

    def aligned(value, step):
        return pl.multiple_of(value * step, step)

    def remote(src, dst, send, recv, device):
        return pltpu.make_async_remote_copy(
            src_ref=src, dst_ref=dst, send_sem=send, recv_sem=recv, device_id=device, device_id_type=MESH
        )

    sent = []
    targets = (1,)

    def start(copy, when=None):
        if when is None:
            copy.start()
        else:
            pl.when(when)(copy.start)
        sent.append((copy, when))

    order = [(s, c, z) for s in range(streams) for c in range(2) for z in range(2)]

    def token_rows(s, c, z):
        return pl.ds((z * 2 + c) * share + s * sub, sub)

    def stream_rows(s):
        return pl.ds(s * sub, sub)

    def columns(j):
        return pl.ds(j * span, span)

    loads = {}

    def load(name, src, dst, when=None):
        copy = pltpu.make_async_copy(src, dst, sem_in.at[len(loads)])
        loads[name] = copy
        if when is None:
            copy.start()
        else:
            pl.when(when)(copy.start)

    my_rows = pl.ds(aligned(core * 2 + chip, sub), sub)
    for s in range(streams):
        load(f"loss{s}", loss_grad.at[stream_rows(s)], up.at[s, my_rows], last)
    load("wd", w_down.at[0], wd)
    load("rows", block_input.at[0], rows_in)
    load("gain", norm_gain, gain)
    for n, key in enumerate(order):
        load(f"gate{n}", gate_act.at[0, token_rows(*key)], gates.at[pl.ds(n * sub, sub)])
    load("wu", w_up.at[0], wu)
    for n, key in enumerate(order):
        src = hidden.at[0, token_rows(*key)]
        load(f"hida{n}", src.at[:, pl.ds(0, cols)], hid_a.at[x, pl.ds(n * sub, sub)])
        load(f"hidb{n}", src.at[:, pl.ds(cols, cols)], hid_b.at[y, pl.ds(n * sub, sub)])

    others = [
        (across, core * 2 + 1 - chip),
        ({"tensor": (1 - chip) * 2 + 1 - core}, (1 - core) * 2 + 1 - chip),
        (mate, (1 - core) * 2 + chip),
    ]

    barrier = pltpu.get_barrier_semaphore()

    def greet(device):
        pl.semaphore_signal(barrier, inc=1, device_id=device, device_id_type=MESH)

    for k in far_first(grid_x):
        greet(at_x(x_peer(k)))
    for k in far_first(grid_y):
        greet(at_y(y_peer(k)))

    @pl.when(jnp.logical_and(pipe < sections - 1, chip == 1))
    def _():
        greet({"pipe": pipe + 1, "tensor": core})
        greet({"pipe": pipe + 1, "tensor": 2 + core})

    for device, _ in others:
        greet(device)

    @pl.when(pipe == 0)
    def _():
        pl.semaphore_wait(barrier, grid_x + grid_y + 1)

    @pl.when(pipe > 0)
    def _():
        pl.semaphore_wait(barrier, grid_x + grid_y + 2)

    @pl.when(last)
    def _():
        for s in range(streams):
            for j in range(chunks):
                remote(
                    loss_grad.at[stream_rows(s), columns(j)], up.at[s, my_rows, columns(j)],
                    send_fwd.at[s, chip, j], sem_block.at[s, chip, j], across,
                ).start()
        for s in range(streams):
            loads[f"loss{s}"].wait()

    for n in range(len(order)):
        loads[f"hida{n}"].wait()
        loads[f"hidb{n}"].wait()
    for k in far_first(grid_x):
        ref = hid_a.at[x]
        start(remote(ref, ref, send_hid.at[k], sem_hid_a.at[x], at_x(x_peer(k))))
    for k in far_first(grid_y):
        ref = hid_b.at[y]
        start(remote(ref, ref, send_hid.at[grid_x + k], sem_hid_b.at[y], at_y(y_peer(k))))

    loads["rows"].wait()
    source = rows_in[...].astype(F32)
    inverse_rms = lax.rsqrt(jnp.mean(source * source, axis=-1, keepdims=True) + EPS_NORM)
    for name in ("wd", "gain", "wu"):
        loads[name].wait()
    for n in range(len(order)):
        loads[f"gate{n}"].wait()

    def block(s, z, c, j):
        return up.at[s, pl.ds(aligned(c * 2 + z, sub), sub), columns(j)]

    def pass_on(s, j):
        for z in range(2):
            ref = block(s, z, core, j)
            forward = remote(ref, ref, send_fwd.at[s, z, j], sem_block.at[s, z, j], across)
            own = jnp.logical_and(last, chip == z)
            pl.when(jnp.logical_not(own))(forward.wait_recv)
            relay = jnp.logical_and(jnp.logical_not(last), chip == 1)
            pl.when(relay)(forward.start)
            sent.append((forward, jnp.logical_or(own, relay)))
            start(remote(ref, ref, send_mate.at[s, z, j], sem_mate.at[s, z, j], mate))

    def multiply(s, j):
        for z in range(2):
            ref = block(s, z, 1 - core, j)
            remote(ref, ref, send_mate.at[s, z, j], sem_mate.at[s, z, j], mate).wait_recv()
        left = up[s, :, columns(j)]
        for n in range(0, units, 256):
            right = pl.ds(n, 256)
            term = jnp.dot(left, wd[columns(j), right], preferred_element_type=F32)
            if j > 0:
                term = term + acc[:, right]
            if j < chunks - 1:
                acc[:, right] = term
            else:
                unit[:, right] = (term * gates[pl.ds(s * stream, stream), right].astype(F32)).astype(BF16)

    def sums(s, i):
        return [
            remote(
                block_send.at[s, pl.ds(aligned(row, sub), sub), columns(i)], block_recv.at[s, n, :, columns(i)],
                send_sum.at[s, n, i], sem_sum.at[s, n, i], device,
            )
            for n, (device, row) in enumerate(others)
        ]

    def second(s, i):
        for n in range(i * span, (i + 1) * span, 256):
            term = lax.dot_general(
                unit[...], wu[pl.ds(n, 256), :], (((1,), (1,)), ((), ())), preferred_element_type=F32
            )
            part[s, :, pl.ds(n, 256)] = term
            block_send[s, :, pl.ds(n, 256)] = term.astype(BF16)
        for copy in sums(s, i):
            start(copy)

    def finish(s):
        rows = stream_rows(s)
        scale = inverse_rms[s * sub : (s + 1) * sub]
        total = jnp.zeros((sub, 1), F32)
        for i in range(chunks):
            normed = part[s, my_rows, columns(i)]
            for n, copy in reversed(list(enumerate(sums(s, i)))):
                copy.wait_recv()
                normed = normed + block_recv[s, n, :, columns(i)].astype(F32)
            value = normed * gain[:, columns(i)]
            scaled[:, columns(i)] = value
            total = total + jnp.sum(rows_in[rows, columns(i)].astype(F32) * value, axis=-1, keepdims=True)
        slope = scale * scale * scale * (total / width)
        for i in range(chunks):
            dx[rows, columns(i)] = (
                up[s, my_rows, columns(i)].astype(F32)
                + scale * scaled[:, columns(i)]
                - rows_in[rows, columns(i)].astype(F32) * slope
            ).astype(BF16)
            for z in targets:
                start(
                    remote(
                        dx.at[rows, columns(i)], up.at[s, my_rows, columns(i)],
                        send_dx.at[s, z, i], sem_block.at[s, chip, i],
                        {"pipe": jnp.maximum(pipe - 1, 0), "tensor": z * 2 + core},
                    ),
                    pipe > 0,
                )

    half_y, half_x = grid_y // 2, grid_x // 2
    my_x, my_y = pl.ds(aligned(x, tokens), tokens), pl.ds(aligned(y, tokens), tokens)
    y_half, x_half = pl.ds(core * half_y, half_y), pl.ds(core * half_x, half_x)
    spread_a = [
        remote(
            up_t.at[x_peer(k), y_half], upt_a.at[y_half, :, my_x], send_upt.at[k], sem_upt_a.at[x], at_x(x_peer(k))
        )
        for k in far_first(grid_x)
    ]
    spread_b = [
        remote(
            up_t.at[x_half, y_peer(k)], upt_b.at[x_half, :, my_y], send_upt.at[grid_x + k], sem_upt_b.at[y],
            at_y(y_peer(k)),
        )
        for k in far_first(grid_y)
    ]

    def spread():
        per = grid_x // 4
        for j in range(4):
            wide = pl.ds(j * (width // 4), width // 4)
            turned = up[:, :, wide].reshape(tokens, width // 4).astype(F32).T.astype(BF16)
            if per:
                up_t[pl.ds(j * per, per)] = turned.reshape(per, grid_y, row_share, tokens)
            else:
                up_t[j // 2, pl.ds((j % 2) * half_y, half_y)] = turned.reshape(half_y, row_share, tokens)
        for n in range(max(grid_x, grid_y) - 1):
            for copies in (spread_a, spread_b):
                if n < len(copies):
                    copies[n].start()
        upt_a[:, :, my_x] = up_t[x]
        upt_b[:, :, my_y] = up_t[:, y]

    for s in range(streams):
        pass_on(s, 0)
        for j in range(chunks):
            if j + 1 < chunks:
                pass_on(s, j + 1)
            multiply(s, j)
        if s == streams - 1:
            pl.when(pipe == 0)(spread)
        for i in range(chunks):
            second(s, i)
        if s > 0:
            finish(s - 1)
    finish(streams - 1)
    outs = [pltpu.make_async_copy(dx, out_dx.at[0], sem_out.at[0])]
    outs[0].start()
    pl.when(pipe > 0)(spread)
    sent.extend((copy, None) for copy in spread_a + spread_b)

    def arrivals(me, size):
        return [lax.rem(me + size - k, size) for k in far_first(size)]

    def lane(slots, part_of, other):
        return slots.at[part_of, :, pl.ds(aligned(other, tokens), tokens)]

    def share_one(slots, mine, sem, mate_sem, send, n, other):
        ref = lane(slots, mine, other)
        copy = remote(ref, ref, send.at[n], sem.at[other], mate)
        copy.wait_recv()
        start(remote(ref, ref, send.at[n], mate_sem.at[other], mate))

    def shared(slots, theirs, mate_sem, send, me, size):
        for n, other in enumerate(arrivals(me, size)):
            ref = lane(slots, theirs, other)
            remote(ref, ref, send.at[n], mate_sem.at[other], mate).wait_recv()

    def gather_wait(slots, sem, me, size):
        for other in arrivals(me, size):
            got = slots.at[other]
            remote(got, got, send_hid.at[0], sem.at[other], mate).wait_recv()

    def contract(slots, hid, grad, gsend, size):
        left = slots[...].reshape(size * row_share, slots.shape[2])
        right = hid[...].reshape(hid.shape[0] * tokens, cols)
        for n in range(0, cols, 256):
            wide = min(256, cols)
            term = jnp.dot(left, right[:, n : n + wide], preferred_element_type=F32)
            term = term.reshape(size, row_share, wide)
            grad[:, :, pl.ds(n, wide)] = term
            gsend[:, :, pl.ds(n, wide)] = term.astype(BF16)

    gather_wait(hid_a, sem_hid_a, x, grid_x)
    gather_wait(hid_b, sem_hid_b, y, grid_y)
    from_x, from_y = arrivals(x, grid_x), arrivals(y, grid_y)
    for n in range(max(len(from_x), len(from_y))):
        if n < len(from_x):
            share_one(upt_a, y_half, sem_upt_a, sem_mate_a, send_upt_mate.at[0], n, from_x[n])
        if n < len(from_y):
            share_one(upt_b, x_half, sem_upt_b, sem_mate_b, send_upt_mate.at[1], n, from_y[n])

    shared(upt_a, pl.ds((1 - core) * half_y, half_y), sem_mate_a, send_upt_mate.at[0], x, grid_x)
    contract(upt_a, hid_a, grad_a, gsend_a, grid_y)
    for k in far_first(grid_y):
        start(
            remote(gsend_a.at[y_peer(k)], grecv_a.at[y], send_grad.at[k], sem_grad_a.at[y], at_y(y_peer(k)))
        )
    shared(upt_b, pl.ds((1 - core) * half_x, half_x), sem_mate_b, send_upt_mate.at[1], y, grid_y)
    contract(upt_b, hid_b, grad_b, gsend_b, grid_x)
    for k in far_first(grid_x):
        start(
            remote(
                gsend_b.at[x_peer(k)], grecv_b.at[x], send_grad.at[grid_y + k], sem_grad_b.at[x], at_x(x_peer(k))
            )
        )

    def total_of(grad, grecv, sem, me, size, offset):
        value = grad[me]
        for other in arrivals(me, size):
            got = grecv.at[other]
            remote(got, got, send_grad.at[0], sem.at[other], mate).wait_recv()
            value = value + grecv[other].astype(F32)
        gradient[:, pl.ds(offset, cols)] = value

    total_of(grad_a, grecv_a, sem_grad_a, y, grid_y, 0)
    total_of(grad_b, grecv_b, sem_grad_b, x, grid_x, cols)
    outs.append(pltpu.make_async_copy(gradient, out_grad, sem_out.at[1]))
    outs[1].start()
    for copy in outs:
        copy.wait()
    for copy, when in sent:
        if when is None:
            copy.wait_send()
        else:
            pl.when(when)(copy.wait_send)


def on_device(grid_x, grid_y, chunks, *args):
    w_up, w_down, gate_act, hidden, block_input, norm_gain, loss_grad, moment_one, moment_two = args
    width, units = w_up.shape[1:]
    tokens = gate_act.shape[1]
    share = tokens // 4
    streams = 2
    stream = tokens // streams
    sub = stream // 4
    cols = units // 2
    row_share = width // (grid_x * grid_y)
    outs = [
        jax.ShapeDtypeStruct(block_input.shape, BF16),
        jax.ShapeDtypeStruct((row_share, units), F32),
    ]
    dma = pltpu.SemaphoreType.DMA
    vmem = pltpu.VMEM
    scratch = [
        vmem((width, units), BF16),
        vmem((width, units), BF16),
        vmem((tokens, units), BF16),
        vmem((share, width), BF16),
        vmem((1, width), F32),
        vmem((streams, stream, width), BF16),
        vmem((grid_x, grid_y, row_share, tokens), BF16),
        vmem((stream, units), F32),
        vmem((stream, units), BF16),
        vmem((streams, stream, width), F32),
        vmem((streams, stream, width), BF16),
        vmem((streams, 3, sub, width), BF16),
        vmem((sub, width), F32),
        vmem((share, width), BF16),
        vmem((grid_x, tokens, cols), BF16),
        vmem((grid_y, tokens, cols), BF16),
        vmem((grid_y, row_share, grid_x * tokens), BF16),
        vmem((grid_x, row_share, grid_y * tokens), BF16),
        vmem((grid_y, row_share, cols), F32),
        vmem((grid_x, row_share, cols), F32),
        vmem((grid_y, row_share, cols), BF16),
        vmem((grid_x, row_share, cols), BF16),
        vmem((grid_y, row_share, cols), BF16),
        vmem((grid_x, row_share, cols), BF16),
        vmem((row_share, units), F32),
        dma((6 + 12 * streams,)),
        dma((2,)),
        dma((streams, 2, chunks)),
        dma((streams, 2, chunks)),
        dma((streams, 3, chunks)),
        dma((grid_x,)),
        dma((grid_y,)),
        dma((grid_x,)),
        dma((grid_y,)),
        dma((grid_x,)),
        dma((grid_y,)),
        dma((grid_y,)),
        dma((grid_x,)),
        dma((streams, 2, chunks)),
        dma((streams, 2, chunks)),
        dma((streams, 3, chunks)),
        dma((streams, 2, chunks)),
        dma((grid_x + grid_y,)),
        dma((grid_x + grid_y,)),
        dma((2, max(grid_x, grid_y))),
        dma((grid_x + grid_y,)),
    ]
    anywhere = pl.BlockSpec(memory_space=pl.ANY)
    input_grad, gradient = pl.pallas_call(
        functools.partial(kernel, grid_x, grid_y, chunks),
        out_shape=outs,
        in_specs=[anywhere] * 7,
        out_specs=[anywhere] * 2,
        scratch_shapes=scratch,
        compiler_params=pltpu.CompilerParams(
            collective_id=0, has_side_effects=True, vmem_limit_bytes=67043328
        ),
    )(*args[:7])
    owner = lax.axis_index("dp")
    current = lax.dynamic_slice_in_dim(w_down[0], owner * row_share, row_share, 0).astype(F32)
    first = BETA_ONE * moment_one[0] + (1.0 - BETA_ONE) * gradient
    second = BETA_TWO * moment_two[0] + (1.0 - BETA_TWO) * gradient * gradient
    direction = first / CORRECT_ONE / (jnp.sqrt(second / CORRECT_TWO) + EPS_ADAM) + DECAY * current
    updated = current - RATE * direction
    return (input_grad, first[None], second[None], updated[None])


def solution(mesh, grid=(8, 8), chunks=2):
    in_specs = (
        P("pipe", None, "tensor"),
        P("pipe", None, "tensor"),
        P("pipe", "dp", "tensor"),
        P("pipe", "dp", "tensor"),
        P("pipe", ("dp", "tensor"), None),
        P("pipe", None),
        P(("dp", "tensor"), None),
        P("pipe", "dp", "tensor"),
        P("pipe", "dp", "tensor"),
    )
    out_specs = (
        P("pipe", ("dp", "tensor"), None),
        P("pipe", "dp", "tensor"),
        P("pipe", "dp", "tensor"),
        P("pipe", "dp", "tensor"),
    )
    return jax.shard_map(
        functools.partial(on_device, *grid, chunks),
        mesh=mesh, in_specs=in_specs, out_specs=out_specs, check_vma=False,
    )
```

time: 118 us -> 110 us (0.932)
  local copies, waits for them, and re-layouts: 6.27 us -> 1.57 us
  Pallas kernels: 110 us -> 106 us
  other arithmetic: 0 us -> 1.87 us
    unnamed x4 -> x1, local copies, waits for them, and re-layouts: 6.27 us -> 1.57 us
    pallas_call x1, Pallas kernels: 110 us -> 106 us  [on_device(): pl.pallas_call(functools.partial(kernel, grid_x, grid_y, chunks), out_sha...]
    broadcast_in_dim x0 -> x1, other arithmetic: none -> 1.87 us  [on_device(): return (input_grad, first[None], second[None], updated[None])]
where the time goes in v2:
time: 110 us
  Pallas kernels  106 us (96%)
  other arithmetic  1.87 us (2%)
  local copies, waits for them, and re-layouts  1.57 us (1%)
    pallas_call x1, Pallas kernels, on_device(): pl.pallas_call(functools.partial(kernel, grid_x, grid_y, chunks), out_sha...  106 us

profile of v2, /device:TPU:1, one launch (start us, length us, event | category | flops | bytes accessed | tf_op | source)
XLA Modules:
  0.0 110.1 jit_solution(18249106188785331212)
XLA Ops:
  0.6 106.0 %shard_map.120 = (bf16[1,32,2048]{2,1,0:T(8,128)(2,1)}, f32[32,1024]{1,0:T(8,128)}) custom-call(bf16[1,2048,1024]{2,1,0:T(8,128)(2,1)} %w_up.1, bf16[1,2048,1024]{2,1,0:T(8,128)(2,1)} %w_down.1, bf16[1,128,1024]{2,1,0:T(8,128)(2,1)} %gate_act.1, bf16[1,128,1024]{2,1,0:T(8,128)(2,1)} %hidden.1, bf16[1,32,2048]{2,1,0:T(8,128)(2,1)} %block_input.1, ...), custom_call_target="tpu_custom_call" | custom-call | tf_op jit(solution)/shard_map/pallas_call | solution.py:456
  106.6 1.9 %fusion.2 = (f32[1,32,1024]{2,1,0:T(8,128)}, f32[1,32,1024]{2,1,0:T(8,128)}, f32[1,32,1024]{2,1,0:T(8,128)}) fusion(bf16[1,2048,1024]{2,1,0:T(8,128)(2,1)} %w_down.1, s32[]{:T(128)S(6)} %select_n.3, f32[32,1024]{1,0:T(8,128)} %get-tuple-element.7, f32[1,32,1024]{2,1,0:T(8,128)} %param.16, f32[1,32,1024]{2,1,0:T(8,128)} %param.17), kind=kLoop, calls=%fused_computation.5 | loop fusion | flops 524288 | bytes 851972 | tf_op jit(solution)/shard_map/broadcast_in_dim | solution.py:472
  108.5 1.6 %copy.14 = bf16[1,32,2048]{2,1,0:T(8,128)(2,1)} copy(bf16[1,32,2048]{2,1,0:T(8,128)(2,1)} %get-tuple-element.15) | data formatting | bytes 262144

commit v3 on v2

--- a/solution.py
+++ b/solution.py
@@ -277,15 +277,19 @@
         for k in far_first(grid_y)
     ]
 
-    def spread():
+    quarters = 4 // chunks
+
+    def turn(chunk):
         per = grid_x // 4
-        for j in range(4):
+        for j in range(chunk * quarters, (chunk + 1) * quarters):
             wide = pl.ds(j * (width // 4), width // 4)
             turned = up[:, :, wide].reshape(tokens, width // 4).astype(F32).T.astype(BF16)
             if per:
                 up_t[pl.ds(j * per, per)] = turned.reshape(per, grid_y, row_share, tokens)
             else:
                 up_t[j // 2, pl.ds((j % 2) * half_y, half_y)] = turned.reshape(half_y, row_share, tokens)
+
+    def spread():
         for n in range(max(grid_x, grid_y) - 1):
             for copies in (spread_a, spread_b):
                 if n < len(copies):
@@ -299,6 +303,8 @@
             if j + 1 < chunks:
                 pass_on(s, j + 1)
             multiply(s, j)
+            if s == streams - 1:
+                pl.when(pipe == 0)(functools.partial(turn, j))
         if s == streams - 1:
             pl.when(pipe == 0)(spread)
         for i in range(chunks):
@@ -308,7 +314,13 @@
     finish(streams - 1)
     outs = [pltpu.make_async_copy(dx, out_dx.at[0], sem_out.at[0])]
     outs[0].start()
-    pl.when(pipe > 0)(spread)
+
+    @pl.when(pipe > 0)
+    def _():
+        for j in range(chunks):
+            turn(j)
+        spread()
+
     sent.extend((copy, None) for copy in spread_a + spread_b)
 
     def arrivals(me, size):
@@ -373,12 +385,14 @@
             got = grecv.at[other]
             remote(got, got, send_grad.at[0], sem.at[other], mate).wait_recv()
             value = value + grecv[other].astype(F32)
-        gradient[:, pl.ds(offset, cols)] = value
+        part_of = pl.ds(offset, cols)
+        gradient[:, part_of] = value
+        copy = pltpu.make_async_copy(gradient.at[:, part_of], out_grad.at[:, part_of], sem_out.at[len(outs)])
+        copy.start()
+        outs.append(copy)
 
     total_of(grad_a, grecv_a, sem_grad_a, y, grid_y, 0)
     total_of(grad_b, grecv_b, sem_grad_b, x, grid_x, cols)
-    outs.append(pltpu.make_async_copy(gradient, out_grad, sem_out.at[1]))
-    outs[1].start()
     for copy in outs:
         copy.wait()
     for copy, when in sent:
@@ -431,7 +445,7 @@
         vmem((grid_x, row_share, cols), BF16),
         vmem((row_share, units), F32),
         dma((6 + 12 * streams,)),
-        dma((2,)),
+        dma((3,)),
         dma((streams, 2, chunks)),
         dma((streams, 2, chunks)),
         dma((streams, 3, chunks)),
@@ -460,9 +474,9 @@
         out_specs=[anywhere] * 2,
         scratch_shapes=scratch,
         compiler_params=pltpu.CompilerParams(
-            collective_id=0, has_side_effects=True, vmem_limit_bytes=67043328
+            collective_id=0, has_side_effects=True, vmem_limit_bytes=48 * 1024 * 1024
         ),
-    )(*args[:7])
+    )(*[pltpu.with_memory_space_constraint(a, pltpu.HBM) for a in args[:7]])
     owner = lax.axis_index("dp")
     current = lax.dynamic_slice_in_dim(w_down[0], owner * row_share, row_share, 0).astype(F32)
     first = BETA_ONE * moment_one[0] + (1.0 - BETA_ONE) * gradient

time: 110 us -> 109 us (level)
  no operation moved by 1% of the time
where the time goes in v3:
time: 109 us
  Pallas kernels  106 us (97%)
  other arithmetic  1.65 us (2%)
    pallas_call x1, Pallas kernels, on_device(): pl.pallas_call(functools.partial(kernel, grid_x, grid_y, chunks), out_sha...  106 us

profile of v3, /device:TPU:1, one launch (start us, length us, event | category | flops | bytes accessed | tf_op | source)
XLA Modules:
  0.0 108.6 jit_solution(2196542570548365440)
XLA Ops:
  0.6 0.0 copy-start
  0.6 0.0 copy-start.1
  0.7 105.6 %shard_map.120 = (bf16[1,32,2048]{2,1,0:T(8,128)(2,1)S(1)}, f32[32,1024]{1,0:T(8,128)S(1)}) custom-call(bf16[1,2048,1024]{2,1,0:T(8,128)(2,1)} %w_up.1, bf16[1,2048,1024]{2,1,0:T(8,128)(2,1)} %w_down.1, bf16[1,128,1024]{2,1,0:T(8,128)(2,1)} %gate_act.1, bf16[1,128,1024]{2,1,0:T(8,128)(2,1)} %hidden.1, bf16[1,32,2048]{2,1,0:T(8,128)(2,1)} %block_input.1, ...), custom_call_target="tpu_custom_call" | custom-call | tf_op jit(solution)/shard_map/pallas_call | solution.py:470
  106.3 0.0 copy-done
  106.3 0.0 copy-done.1
  106.3 1.6 %fusion.2 = (f32[1,32,1024]{2,1,0:T(8,128)}, f32[1,32,1024]{2,1,0:T(8,128)}, f32[1,32,1024]{2,1,0:T(8,128)}) fusion(bf16[1,2048,1024]{2,1,0:T(8,128)(2,1)} %w_down.1, s32[]{:T(128)S(6)} %select_n.3, f32[32,1024]{1,0:T(8,128)S(1)} %get-tuple-element.7, f32[1,32,1024]{2,1,0:T(8,128)S(1)} %copy-done, f32[1,32,1024]{2,1,0:T(8,128)S(1)} %copy-done.1), kind=kLoop, calls=%fused_computation.5 | loop fusion | flops 524288 | bytes 851972 | tf_op jit(solution)/shard_map/broadcast_in_dim | solution.py:486
  108.0 0.7 copy.14
Async XLA Ops:
  0.6 105.7 %copy-start = (f32[1,32,1024]{2,1,0:T(8,128)S(1)}, f32[1,32,1024]{2,1,0:T(8,128)}, u32[]{:S(2)}) copy-start(f32[1,32,1024]{2,1,0:T(8,128)} %param.16) | copy-start | bytes 393220
  0.6 105.7 %copy-start.1 = (f32[1,32,1024]{2,1,0:T(8,128)S(1)}, f32[1,32,1024]{2,1,0:T(8,128)}, u32[]{:S(2)}) copy-start(f32[1,32,1024]{2,1,0:T(8,128)} %param.17) | copy-start | bytes 393220
